TPU v7x, 128 devices: a whole 4x4x4 slice. The times are simulated.
128 devices in a mesh: lat: 16 (over x, z), dep: 8 (over y, core).
Axes of the slice: x: 4, y: 4, z: 4, core: 2. Of those that a mesh axis runs over, the one named last changes fastest.
Arguments:
- state: float32 [64, 64, 128], P('lat', 'dep'), may hold values from 0.2 to 1
- kappa: float32 [64, 64, 128], P('lat', 'dep'), may hold values from 0.3 to 3
- rate: float32 [64, 64], P('lat', 'dep'), may hold values from 1 to 4
- grads: float32 [3, 64, 64], replicated, may hold values from -0.75 to 0.75
- lift: float32 [4, 32, 128], replicated, may hold values from -0.375 to 0.375
- rhs: float32 [64, 64, 32, 128], P('lat', 'dep'), may hold values from -18 to 18
Outputs:
- update: float32 [64, 64, 32, 128], P('lat', 'dep')
All inputs are finite; a program needn't handle non-finite values.
Results may differ from a plain program's by a relative error of at most 0.0003.
Values sent between devices are 32-bit elements; how exact they have to be, the bound alone decides.
A program may use at most 128 MiB of HBM per device.

v0:
```python
import jax
import jax.numpy as jnp
from jax import lax
from jax.sharding import PartitionSpec as P

KRY = 8
highest = lax.Precision.HIGHEST
mass_shift = 0.25


def with_halo(cells, sides, width, closed):
    for axis, dim in sides:
        count = lax.axis_size(axis)
        ends = count if closed else count - 1
        head = lax.slice_in_dim(cells, 0, width, axis=dim)
        tail = lax.slice_in_dim(cells, cells.shape[dim] - width, cells.shape[dim], axis=dim)
        cells = jnp.concatenate(
            [
                lax.ppermute(tail, axis, [(i, (i + 1) % count) for i in range(ends)]),
                cells,
                lax.ppermute(head, axis, [((i + 1) % count, i) for i in range(ends)]),
            ],
            axis=dim,
        )
    return cells


def from_behind(value, axis, steps):
    count = lax.axis_size(axis)
    pairs = [(source, (source + steps) % count) for source in range(count)]
    return lax.ppermute(value, axis, pairs)


def passed_along(array, axis, by):
    peers = lax.axis_size(axis)
    pairs = [(i, i + by) for i in range(peers) if 0 <= i + by < peers]
    return lax.ppermute(array, axis, pairs)


def face_table():
    unknown = jnp.arange(128, dtype=jnp.int32)[:, None]
    column = jnp.arange(128, dtype=jnp.int32)[None, :]
    face_id = column // 32
    species = column // 16 % 2
    along_one = column % 16 // 4
    along_two = column % 4
    edge_pos = 3 * (face_id % 2)
    is_lateral = face_id < 2
    node_x = jnp.where(is_lateral, edge_pos, along_one)
    node_y = jnp.where(is_lateral, along_one, along_two)
    node_z = jnp.where(is_lateral, along_two, edge_pos)
    target = species * 64 + node_x * 16 + node_y * 4 + node_z
    return (unknown == target).astype(jnp.float32)


def pairing_table():
    unknown = jnp.arange(128, dtype=jnp.int32)
    return (unknown[:, None] % 64 == unknown[None, :] % 64).astype(jnp.float32)


def element_tiles(kappa_rows, state_rows, rate_rows, grads, select):
    row_count = kappa_rows.shape[0]
    split_kappa = kappa_rows.reshape(row_count, 2, 64)
    stiffness = jnp.einsum("dqi,nsq,dqj->nsij", grads, split_kappa, grads, precision=highest)
    zero_block = jnp.zeros((row_count, 64, 64), jnp.float32)
    top_half = jnp.concatenate([stiffness[:, 0], zero_block], axis=2)
    bottom_half = jnp.concatenate([zero_block, stiffness[:, 1]], axis=2)
    face_kappa = jnp.dot(kappa_rows, select, precision=highest)
    penalty = jnp.dot(face_kappa, select.T, precision=highest)
    partner = jnp.concatenate([state_rows[:, 64:], state_rows[:, :64]], axis=1)
    identity = jnp.eye(128, dtype=jnp.float32)
    diag_tiles = jnp.concatenate([top_half, bottom_half], axis=1)
    diag_tiles = diag_tiles + identity[None] * (mass_shift + penalty)[:, None, :]
    diag_tiles = diag_tiles + pairing_table()[None] * (rate_rows[:, None] * partner)[:, None, :]
    return (diag_tiles, face_kappa)


def apply_operator(vectors, diag_tiles, couple, select):
    lat_rows = vectors.shape[0]
    dep_rows = vectors.shape[1]
    columns = vectors.shape[2]
    traces = jnp.einsum("aevu,uk->aevk", vectors, select, precision=highest)
    lat_rims = jnp.stack([traces[0, :, :, 0:32], traces[-1, :, :, 32:64]]).reshape(
        2, dep_rows, columns * 32
    )
    lat_wide = with_halo(lat_rims, (("lat", 0),), 1, True)
    prev_lat = lat_wide[0].reshape(dep_rows, columns, 32)
    next_lat = lat_wide[3].reshape(dep_rows, columns, 32)
    dep_rims = jnp.stack([traces[:, 0, :, 64:96], traces[:, -1, :, 96:128]]).reshape(
        2, lat_rows, columns * 32
    )
    dep_wide = with_halo(dep_rims, (("dep", 0),), 1, False)
    prev_dep = dep_wide[0].reshape(lat_rows, columns, 32)
    next_dep = dep_wide[3].reshape(lat_rows, columns, 32)
    from_left = jnp.concatenate([prev_lat[None], traces[:-1, :, :, 32:64]], axis=0)
    from_right = jnp.concatenate([traces[1:, :, :, 0:32], next_lat[None]], axis=0)
    from_below = jnp.concatenate([prev_dep[:, None], traces[:, :-1, :, 96:128]], axis=1)
    from_above = jnp.concatenate([traces[:, 1:, :, 64:96], next_dep[:, None]], axis=1)
    near_traces = jnp.concatenate([from_left, from_right, from_below, from_above], axis=-1)
    own_part = jnp.einsum("aeij,aevj->aevi", diag_tiles, vectors, precision=highest)
    coupled = jnp.einsum("aeki,aevk->aevi", couple, near_traces, precision=highest)
    return own_part - coupled


def inner_local(left_block, right_block):
    return jnp.einsum("aevu,aewu->vw", left_block, right_block, precision=highest)


def combine_columns(vectors, matrix):
    return jnp.einsum("aevu,vw->aewu", vectors, matrix, precision=highest)


def factor(gram_matrix):
    lower_factor = jnp.linalg.cholesky(gram_matrix)
    identity = jnp.eye(gram_matrix.shape[0], dtype=gram_matrix.dtype)
    inverse = jax.scipy.linalg.solve_triangular(lower_factor, identity, lower=True)
    return (lower_factor.T, inverse.T)


def per_device(state, kappa, rate, grads, lift, rhs):
    select = face_table()

    def one_row(row_data):
        return element_tiles(row_data[0], row_data[1], row_data[2], grads, select)

    diag_tiles, face_kappa = lax.map(one_row, (kappa, state, rate))
    lat_end = face_kappa[-1, :, 32:64]
    dep_end = face_kappa[:, -1, 96:128]
    own_right = lift[1] * face_kappa[:, :, 32:64, None]
    own_top = lift[3] * face_kappa[:, :, 96:128, None]
    sent_lat = from_behind(lift[0][None] * lat_end[:, :, None], "lat", 1)
    sent_dep = passed_along(lift[2][None] * dep_end[:, :, None], "dep", 1)
    left_tiles = jnp.concatenate(
        [sent_lat[None], lift[0] * face_kappa[:-1, :, 32:64, None]], axis=0
    )
    below_tiles = jnp.concatenate(
        [sent_dep[:, None], lift[2] * face_kappa[:, :-1, 96:128, None]], axis=1
    )
    couple = jnp.concatenate([left_tiles, own_right, below_tiles, own_top], axis=2)
    columns = rhs.shape[2]
    start_factor, inverse = factor(lax.psum(inner_local(rhs, rhs), ("lat", "dep")))
    basis_list = [combine_columns(rhs, inverse)]
    coef_table = []
    for step_index in range(KRY):
        image_block = apply_operator(basis_list[step_index], diag_tiles, couple, select)
        local_prods = jnp.stack(
            [inner_local(basis_list[prior], image_block) for prior in range(step_index + 1)]
        )
        coef_stack = lax.psum(local_prods, ("lat", "dep"))
        for prior in range(step_index + 1):
            image_block = image_block - combine_columns(basis_list[prior], coef_stack[prior])
        gram_matrix = lax.psum(inner_local(image_block, image_block), ("lat", "dep"))
        upper_factor, inverse = factor(gram_matrix)
        column_coefs = [coef_stack[prior] for prior in range(step_index + 1)]
        column_coefs.append(upper_factor)
        coef_table.append(column_coefs)
        basis_list.append(combine_columns(image_block, inverse))
    zero_small = jnp.zeros((columns, columns), jnp.float32)
    block_rows = []
    for row_index in range(KRY + 1):
        row_blocks = []
        for col_index in range(KRY):
            if row_index <= col_index + 1:
                row_blocks.append(coef_table[col_index][row_index])
            else:
                row_blocks.append(zero_small)
        block_rows.append(jnp.concatenate(row_blocks, axis=1))
    hessenberg = jnp.concatenate(block_rows, axis=0)
    gram_small = jnp.dot(hessenberg.T, hessenberg, precision=highest)
    right_side = jnp.dot(hessenberg[:columns].T, start_factor, precision=highest)
    coeffs = jax.scipy.linalg.cho_solve((jnp.linalg.cholesky(gram_small), True), right_side)
    update = combine_columns(basis_list[0], coeffs[:columns])
    for step_index in range(1, KRY):
        update = update + combine_columns(
            basis_list[step_index], coeffs[step_index * columns : (step_index + 1) * columns]
        )
    return update


def solution(mesh):
    in_specs = (
        P("lat", "dep", None),
        P("lat", "dep", None),
        P("lat", "dep"),
        P(),
        P(),
        P("lat", "dep", None, None),
    )
    out_specs = P("lat", "dep", None, None)
    return jax.shard_map(
        per_device, mesh=mesh, in_specs=in_specs, out_specs=out_specs, check_vma=False
    )
```

profile of v0, /device:TPU:1, one launch (start us, length us, event | category | flops | bytes accessed | tf_op | source)
XLA Modules:
  0.0 1614.5 jit_solution(5282608771596217027)
XLA Ops:
  1.6 68.8 %psum.119 = f32[32,32]{0,1:T(8,128)S(1)} all-reduce(f32[32,32]{0,1:T(8,128)S(1)} %convolution_bitcast_fusion.97), channel_id=1, replica_groups=mesh['lat'=16,'dep'=8] {'lat','dep'}, use_global_device_ids=true, to_apply=%region_0.1 | all-reduce | flops 1024 | bytes 8192 | tf_op jit(solution)/shard_map/psum | solution.py:141
  79.8 4.8 collective-permute-start.1
  91.2 50.8 %while.18 = (s32[]{:T(128)}, f32[4,8,128,128]{3,2,1,0:T(8,128)S(1)}, f32[4,8,128]{2,1,0:T(8,128)S(1)}, f32[3,64,64]{2,0,1:T(4,128)S(1)}, f32[4,8,128]{2,1,0:T(8,...) while((s32[]{:T(128)}, ...), condition=%wide.region_4.7_spmd.clone.clone, body=%wide.region_3.6_spmd.clone.clone.sunk | while | flops 63704832 | bytes 7220429 | solution.py:126
  172.6 65.2 %psum.120 = f32[32,32]{0,1:T(8,128)S(1)} all-reduce(f32[32,32]{0,1:T(8,128)} %convolution_bitcast_fusion.95), channel_id=1, replica_groups=mesh['lat'=16,'dep'=8] {'lat','dep'}, use_global_device_ids=true, to_apply=%region_5.8 | all-reduce | flops 1024 | bytes 8192 | tf_op jit(solution)/shard_map/psum | solution.py:149
  240.1 64.2 %psum.121 = f32[32,32]{0,1:T(8,128)S(1)} all-reduce(f32[32,32]{0,1:T(8,128)S(1)} %convolution_bitcast_fusion.94), channel_id=1, replica_groups=mesh['lat'=16,'dep'=8] {'lat','dep'}, use_global_device_ids=true, to_apply=%region_6.9 | all-reduce | flops 1024 | bytes 8192 | tf_op jit(solution)/shard_map/psum | solution.py:152
  322.7 4.8 collective-permute-start.7
  344.4 62.0 %psum.122 = f32[2,32,32]{1,2,0:T(8,128)S(1)} all-reduce(f32[2,32,32]{1,2,0:T(8,128)S(1)} %pad_maximum_fusion.5), channel_id=1, replica_groups=mesh['lat'=16,'dep'=8] {'lat','dep'}, use_global_device_ids=true, to_apply=%region_7.10 | all-reduce | flops 2048 | bytes 16384 | tf_op jit(solution)/shard_map/psum | solution.py:149
  410.1 63.5 %psum.123 = f32[32,32]{0,1:T(8,128)S(1)} all-reduce(f32[32,32]{0,1:T(8,128)S(1)} %convolution_bitcast_fusion.90), channel_id=1, replica_groups=mesh['lat'=16,'dep'=8] {'lat','dep'}, use_global_device_ids=true, to_apply=%region_8.11 | all-reduce | flops 1024 | bytes 8192 | tf_op jit(solution)/shard_map/psum | solution.py:152
  490.8 4.8 collective-permute-start.11
  507.8 4.3 convolution_subtract_fusion.5
  513.9 62.9 %psum.124 = f32[3,32,32]{1,2,0:T(8,128)S(1)} all-reduce(f32[3,32,32]{1,2,0:T(8,128)S(1)} %pad_maximum_fusion.4), channel_id=1, replica_groups=mesh['lat'=16,'dep'=8] {'lat','dep'}, use_global_device_ids=true, to_apply=%region_9.12 | all-reduce | flops 3072 | bytes 24576 | tf_op jit(solution)/shard_map/psum | solution.py:149
  581.1 64.3 %psum.125 = f32[32,32]{0,1:T(8,128)S(1)} all-reduce(f32[32,32]{0,1:T(8,128)S(1)} %convolution_bitcast_fusion.85), channel_id=1, replica_groups=mesh['lat'=16,'dep'=8] {'lat','dep'}, use_global_device_ids=true, to_apply=%region_10.13 | all-reduce | flops 1024 | bytes 8192 | tf_op jit(solution)/shard_map/psum | solution.py:152
  662.6 4.8 collective-permute-start.15
  685.9 63.0 %psum.126 = f32[4,32,32]{1,2,0:T(8,128)S(1)} all-reduce(f32[4,32,32]{1,2,0:T(8,128)S(1)} %pad_maximum_fusion.3), channel_id=1, replica_groups=mesh['lat'=16,'dep'=8] {'lat','dep'}, use_global_device_ids=true, to_apply=%region_11.14 | all-reduce | flops 4096 | bytes 32768 | tf_op jit(solution)/shard_map/psum | solution.py:149
  753.7 63.5 %psum.127 = f32[32,32]{0,1:T(8,128)S(1)} all-reduce(f32[32,32]{0,1:T(8,128)S(1)} %convolution_bitcast_fusion.79), channel_id=1, replica_groups=mesh['lat'=16,'dep'=8] {'lat','dep'}, use_global_device_ids=true, to_apply=%region_12.15 | all-reduce | flops 1024 | bytes 8192 | tf_op jit(solution)/shard_map/psum | solution.py:152
  836.5 4.8 collective-permute-start.19
  860.7 62.7 %psum.128 = f32[5,32,32]{1,2,0:T(8,128)S(1)} all-reduce(f32[5,32,32]{1,2,0:T(8,128)S(1)} %fusion.76), channel_id=1, replica_groups=mesh['lat'=16,'dep'=8] {'lat','dep'}, use_global_device_ids=true, to_apply=%region_13.16 | all-reduce | flops 5120 | bytes 40960 | tf_op jit(solution)/shard_map/psum | solution.py:149
  928.8 64.2 %psum.129 = f32[32,32]{0,1:T(8,128)S(1)} all-reduce(f32[32,32]{0,1:T(8,128)S(1)} %convolution_bitcast_fusion.72), channel_id=1, replica_groups=mesh['lat'=16,'dep'=8] {'lat','dep'}, use_global_device_ids=true, to_apply=%region_14.17 | all-reduce | flops 1024 | bytes 8192 | tf_op jit(solution)/shard_map/psum | solution.py:152
  1011.7 4.8 collective-permute-start.23
  1036.6 63.3 %psum.130 = f32[6,32,32]{1,2,0:T(8,128)S(1)} all-reduce(f32[6,32,32]{1,2,0:T(8,128)S(1)} %fusion.70), channel_id=1, replica_groups=mesh['lat'=16,'dep'=8] {'lat','dep'}, use_global_device_ids=true, to_apply=%region_15.18 | all-reduce | flops 6144 | bytes 49152 | tf_op jit(solution)/shard_map/psum | solution.py:149
  1106.0 63.8 %psum.131 = f32[32,32]{0,1:T(8,128)S(1)} all-reduce(f32[32,32]{0,1:T(8,128)S(1)} %convolution_bitcast_fusion.64), channel_id=1, replica_groups=mesh['lat'=16,'dep'=8] {'lat','dep'}, use_global_device_ids=true, to_apply=%region_16.19 | all-reduce | flops 1024 | bytes 8192 | tf_op jit(solution)/shard_map/psum | solution.py:152
  1189.3 4.8 collective-permute-start.27
  1214.6 63.2 %psum.132 = f32[7,32,32]{1,2,0:T(8,128)S(1)} all-reduce(f32[7,32,32]{1,2,0:T(8,128)S(1)} %fusion.63), channel_id=1, replica_groups=mesh['lat'=16,'dep'=8] {'lat','dep'}, use_global_device_ids=true, to_apply=%region_17.20 | all-reduce | flops 7168 | bytes 57344 | tf_op jit(solution)/shard_map/psum | solution.py:149
  1284.5 64.2 %psum.133 = f32[32,32]{0,1:T(8,128)S(1)} all-reduce(f32[32,32]{0,1:T(8,128)S(1)} %convolution_bitcast_fusion.55), channel_id=1, replica_groups=mesh['lat'=16,'dep'=8] {'lat','dep'}, use_global_device_ids=true, to_apply=%region_18.21 | all-reduce | flops 1024 | bytes 8192 | tf_op jit(solution)/shard_map/psum | solution.py:152
  1367.0 4.8 collective-permute-start.31
  1390.9 63.0 %psum.134 = f32[8,32,32]{1,2,0:T(8,128)S(1)} all-reduce(f32[8,32,32]{1,2,0:T(8,128)S(1)} %fusion.55), channel_id=1, replica_groups=mesh['lat'=16,'dep'=8] {'lat','dep'}, use_global_device_ids=true, to_apply=%region_19.22 | all-reduce | flops 8192 | bytes 65536 | tf_op jit(solution)/shard_map/psum | solution.py:149
  1459.3 63.7 %psum.135 = f32[32,32]{0,1:T(8,128)S(1)} all-reduce(f32[32,32]{0,1:T(8,128)S(1)} %convolution_bitcast_fusion.45), channel_id=1, replica_groups=mesh['lat'=16,'dep'=8] {'lat','dep'}, use_global_device_ids=true, to_apply=%region_20.23 | all-reduce | flops 1024 | bytes 8192 | tf_op jit(solution)/shard_map/psum | solution.py:152
  1536.6 11.7 cholesky.77
  1551.2 9.8 custom-call.23
  1563.2 11.7 cholesky.132
  1579.7 5.1 while.17
  1584.8 20.8 %custom-call.24 = f32[2,128,128]{1,2,0:T(8,128)S(1)} custom-call(f32[2,128,128]{2,1,0:T(8,128)} %get-tuple-element.122), custom_call_target="InvertDiagBlocksLowerTriangular" | custom-call | tf_op jit(solution)/shard_map/jit(_cho_solve)/triangular_solve | solution.py:171
  (677 shorter events, 427.5 us)
Async XLA Ops:
  79.1 84.4 %collective-permute-start = (f32[1,8,1024]{2,1,0:T(8,128)}, f32[1,8,1024]{2,1,0:T(8,128)}, u32[]{:S(2)}, u32[]{:S(2)}) collective-permute-start(f32[1,8,1024]{2,1,0:T(8,128)} %slice.619), channel_id=1, source_target_pairs={{0,8},{8,16},{16,24},{24,32},{32,40},{40,48},{48,56},{56,64},{64,7... | collective-permute-start | bytes 98312 | tf_op jit(solution)/shard_map/ppermute | solution.py:19
  79.8 85.2 %collective-permute-start.1 = (f32[1,8,1024]{2,1,0:T(8,128)}, f32[1,8,1024]{2,1,0:T(8,128)}, u32[]{:S(2)}, u32[]{:S(2)}) collective-permute-start(f32[1,8,1024]{2,1,0:T(8,128)} %slice.623), channel_id=1, source_target_pairs={{8,0},{16,8},{24,16},{32,24},{40,32},{48,40},{56,48},{64,56},{72,6... | collective-permute-start | bytes 98312 | tf_op jit(solution)/shard_map/ppermute | solution.py:21
  85.4 70.7 %collective-permute-start.2 = (f32[1,4,1024]{2,1,0:T(4,128)}, f32[1,4,1024]{2,1,0:T(4,128)S(1)}, u32[]{:S(2)}, u32[]{:S(2)}) collective-permute-start(f32[1,4,1024]{2,1,0:T(4,128)} %slice.625), channel_id=1, source_target_pairs={{0,1},{1,2},{2,3},{3,4},{4,5},{5,6},{6,7},{8,9},{9,10},{10,11},{11... | collective-permute-start | bytes 49160 | tf_op jit(solution)/shard_map/ppermute | solution.py:19
  89.1 73.0 %collective-permute-start.3 = (f32[1,4,1024]{2,1,0:T(4,128)}, f32[1,4,1024]{2,1,0:T(4,128)}, u32[]{:S(2)}, u32[]{:S(2)}) collective-permute-start(f32[1,4,1024]{2,1,0:T(4,128)} %slice.629), channel_id=1, source_target_pairs={{1,0},{2,1},{3,2},{4,3},{5,4},{6,5},{7,6},{9,8},{10,9},{11,10},{12... | collective-permute-start | bytes 49160 | tf_op jit(solution)/shard_map/ppermute | solution.py:21
  142.8 23.7 %collective-permute-start.4 = (f32[8,32,128]{2,1,0:T(8,128)}, f32[8,32,128]{2,1,0:T(8,128)}, u32[]{:S(2)}, u32[]{:S(2)}) collective-permute-start(f32[8,32,128]{2,1,0:T(8,128)} %broadcast_multiply_fusion.4), channel_id=1, source_target_pairs={{0,8},{8,16},{16,24},{24,32},{32,40},{40,48},{48,56},{56,64},{64,7... | collective-permute-start | bytes 393224 | tf_op jit(solution)/shard_map/ppermute | solution.py:31
  156.0 10.5 collective-permute-start.5
  321.9 15.0 collective-permute-start.6
  322.7 15.2 collective-permute-start.7
  327.5 5.6 collective-permute-start.8
  331.2 5.1 collective-permute-start.9
  490.7 16.1 collective-permute-start.10
  490.8 16.1 collective-permute-start.11
  496.6 8.8 collective-permute-start.12
  500.7 5.4 collective-permute-start.13
  662.5 15.7 collective-permute-start.14
  662.6 15.7 collective-permute-start.15
  668.4 8.4 collective-permute-start.16
  672.2 5.2 collective-permute-start.17
  835.8 15.8 collective-permute-start.18
  836.5 15.9 collective-permute-start.19
  842.2 7.7 collective-permute-start.20
  845.9 5.1 collective-permute-start.21
  1010.9 16.1 collective-permute-start.22
  1011.7 16.1 collective-permute-start.23
  1017.4 7.6 collective-permute-start.24
  1021.2 5.1 collective-permute-start.25
  1188.5 15.9 collective-permute-start.26
  1189.3 16.0 collective-permute-start.27
  1195.0 6.5 collective-permute-start.28
  1366.7 14.9 collective-permute-start.30
  1367.0 14.8 collective-permute-start.31
  1372.7 7.2 collective-permute-start.32
  (93 other events, 1334.6 us)
where the time goes:
time: 1630 us; the launch traced here: 1610 us
  blocking collectives  1090 us (67%)
  matrix products  178 us (11%)
  other arithmetic  138 us (8%)
  local copies, waits for them, and re-layouts  118 us (7%)
  starting transfers between devices  83.3 us (5%)
    psum x8, blocking collectives, per_device(): lax.psum(inner_local(image_block, image_block), ('lat', 'dep'))  511 us
    psum x8, blocking collectives, per_device(): coef_stack = lax.psum(local_prods, ('lat', 'dep'))  505 us
    psum x1, blocking collectives, per_device(): lax.psum(inner_local(rhs, rhs), ('lat', 'dep'))  68.8 us
    ppermute x16, starting transfers between devices, with_halo(): lax.ppermute(head, axis, [((i + 1) % count, i) for i in range(ends)])  54.5 us
    dot_general x52, matrix products, combine_columns(): return jnp.einsum('aevu,vw->aewu', vectors, matrix, precision=highest)  46.2 us
    another operation x7, other arithmetic, per_device(): jnp.linalg.cholesky(gram_small)  35.7 us
    dot_general x8, matrix products, apply_operator(): jnp.einsum('aeki,aevk->aevi', couple, near_traces, precision=highest)  34.6 us
    dot_general x8, matrix products, apply_operator(): jnp.einsum('aeij,aevj->aevi', diag_tiles, vectors, precision=highest)  33.2 us
  transfers between devices with their start and end apart: 34, of which 5 were waited for; matrix products, arithmetic and copies ran while one was open for 7% of the time, Pallas kernels for 0%

commit v1 on v0

--- a/solution.py
+++ b/solution.py
@@ -149,7 +149,9 @@
         coef_stack = lax.psum(local_prods, ("lat", "dep"))
         for prior in range(step_index + 1):
             image_block = image_block - combine_columns(basis_list[prior], coef_stack[prior])
-        gram_matrix = lax.psum(inner_local(image_block, image_block), ("lat", "dep"))
+        gram_matrix = jnp.sum(
+            lax.all_gather(inner_local(image_block, image_block), axis_name=("lat", "dep")), axis=0
+        )
         upper_factor, inverse = factor(gram_matrix)
         column_coefs = [coef_stack[prior] for prior in range(step_index + 1)]
         column_coefs.append(upper_factor)

time: 1630 us -> 1440 us (0.88)
  blocking collectives: 1090 us -> 885 us
    psum x8 -> x0, blocking collectives: 511 us -> none  [per_device(): lax.psum(inner_local(image_block, image_block), ('lat', 'dep'))]
    all_gather x0 -> x8, blocking collectives: none -> 310 us  [per_device(): lax.all_gather(inner_local(image_block, image_block), axis_name=('lat', '...]
  transfers between devices with their start and end apart: 34 -> 34, of which waited for: 5 -> 5; matrix products, arithmetic and copies ran while one was open for 7% -> 8% of each run, Pallas kernels for 0% -> 0%
where the time goes in v1:
time: 1440 us; the launch traced here: 1430 us
  blocking collectives  885 us (61%)
  matrix products  178 us (12%)
  other arithmetic  151 us (10%)
  local copies, waits for them, and re-layouts  118 us (8%)
  starting transfers between devices  85.4 us (6%)
    psum x8, blocking collectives, per_device(): coef_stack = lax.psum(local_prods, ('lat', 'dep'))  507 us
    all_gather x8, blocking collectives, per_device(): lax.all_gather(inner_local(image_block, image_block), axis_name=('lat', '...  310 us
    psum x1, blocking collectives, per_device(): lax.psum(inner_local(rhs, rhs), ('lat', 'dep'))  68.8 us
    ppermute x16, starting transfers between devices, with_halo(): lax.ppermute(head, axis, [((i + 1) % count, i) for i in range(ends)])  51.7 us
    dot_general x52, matrix products, combine_columns(): return jnp.einsum('aevu,vw->aewu', vectors, matrix, precision=highest)  46.2 us
    another operation x7, other arithmetic, per_device(): jnp.linalg.cholesky(gram_small)  35.9 us
    dot_general x8, matrix products, apply_operator(): jnp.einsum('aeki,aevk->aevi', couple, near_traces, precision=highest)  34.6 us
    dot_general x8, matrix products, apply_operator(): jnp.einsum('aeij,aevj->aevi', diag_tiles, vectors, precision=highest)  33.3 us
  transfers between devices with their start and end apart: 34, of which 5 were waited for; matrix products, arithmetic and copies ran while one was open for 8% of the time, Pallas kernels for 0%

profile of v1, /device:TPU:1, one launch (start us, length us, event | category | flops | bytes accessed | tf_op | source)
XLA Modules:
  0.0 1428.5 jit_solution(15465172937849154641)
XLA Ops:
  1.6 68.8 %psum.63 = f32[32,32]{0,1:T(8,128)S(1)} all-reduce(f32[32,32]{0,1:T(8,128)S(1)} %convolution_bitcast_fusion.97), channel_id=1, replica_groups=mesh['lat'=16,'dep'=8] {'lat','dep'}, use_global_device_ids=true, to_apply=%region_0.1 | all-reduce | flops 1024 | bytes 8192 | tf_op jit(solution)/shard_map/psum | solution.py:141
  79.9 4.8 collective-permute-start.1
  91.3 50.8 %while.18 = (s32[]{:T(128)}, f32[4,8,128,128]{3,2,1,0:T(8,128)S(1)}, f32[4,8,128]{2,1,0:T(8,128)S(1)}, f32[3,64,64]{2,0,1:T(4,128)S(1)}, f32[4,8,128]{2,1,0:T(8,...) while((s32[]{:T(128)}, ...), condition=%wide.region_4.7_spmd.clone.clone, body=%wide.region_3.6_spmd.clone.clone.sunk | while | flops 63704832 | bytes 7220429 | solution.py:126
  167.7 4.3 convolution_subtract_fusion.7
  173.2 65.2 %psum.64 = f32[32,32]{0,1:T(8,128)S(1)} all-reduce(f32[32,32]{0,1:T(8,128)} %convolution_bitcast_fusion.95), channel_id=1, replica_groups=mesh['lat'=16,'dep'=8] {'lat','dep'}, use_global_device_ids=true, to_apply=%region_5.8 | all-reduce | flops 1024 | bytes 8192 | tf_op jit(solution)/shard_map/psum | solution.py:149
  240.6 38.7 %all-gather = f32[4096,32]{1,0:T(8,128)} all-gather(f32[32,32]{1,0:T(8,128)S(1)} %convolution_bitcast_fusion.94), channel_id=2, replica_groups=mesh['lat'=16,'dep'=8] {'lat','dep'}, dimensions={0}, use_global_device_ids=true | all-gather | bytes 528384 | tf_op jit(solution)/shard_map/all_gather | solution.py:153
  314.9 4.3 convolution_subtract_fusion.6
  320.6 62.5 %psum.65 = f32[2,32,32]{1,2,0:T(8,128)S(1)} all-reduce(f32[2,32,32]{1,2,0:T(8,128)S(1)} %pad_maximum_fusion.5), channel_id=1, replica_groups=mesh['lat'=16,'dep'=8] {'lat','dep'}, use_global_device_ids=true, to_apply=%region_7.10 | all-reduce | flops 2048 | bytes 16384 | tf_op jit(solution)/shard_map/psum | solution.py:149
  386.7 38.6 %all-gather.1 = f32[4096,32]{1,0:T(8,128)} all-gather(f32[32,32]{1,0:T(8,128)S(1)} %convolution_bitcast_fusion.90), channel_id=3, replica_groups=mesh['lat'=16,'dep'=8] {'lat','dep'}, dimensions={0}, use_global_device_ids=true | all-gather | bytes 528384 | tf_op jit(solution)/shard_map/all_gather | solution.py:153
  461.5 4.3 convolution_subtract_fusion.5
  467.7 63.4 %psum.66 = f32[3,32,32]{1,2,0:T(8,128)S(1)} all-reduce(f32[3,32,32]{1,2,0:T(8,128)S(1)} %pad_maximum_fusion.4), channel_id=1, replica_groups=mesh['lat'=16,'dep'=8] {'lat','dep'}, use_global_device_ids=true, to_apply=%region_9.12 | all-reduce | flops 3072 | bytes 24576 | tf_op jit(solution)/shard_map/psum | solution.py:149
  535.2 38.6 %all-gather.2 = f32[4096,32]{1,0:T(8,128)} all-gather(f32[32,32]{1,0:T(8,128)S(1)} %convolution_bitcast_fusion.85), channel_id=4, replica_groups=mesh['lat'=16,'dep'=8] {'lat','dep'}, dimensions={0}, use_global_device_ids=true | all-gather | bytes 528384 | tf_op jit(solution)/shard_map/all_gather | solution.py:153
  592.7 4.7 collective-permute-start.15
  609.3 4.3 convolution_subtract_fusion.4
  616.0 63.0 %psum.67 = f32[4,32,32]{1,2,0:T(8,128)S(1)} all-reduce(f32[4,32,32]{1,2,0:T(8,128)S(1)} %pad_maximum_fusion.3), channel_id=1, replica_groups=mesh['lat'=16,'dep'=8] {'lat','dep'}, use_global_device_ids=true, to_apply=%region_11.14 | all-reduce | flops 4096 | bytes 32768 | tf_op jit(solution)/shard_map/psum | solution.py:149
  683.9 38.6 %all-gather.3 = f32[4096,32]{1,0:T(8,128)} all-gather(f32[32,32]{1,0:T(8,128)S(1)} %convolution_bitcast_fusion.79), channel_id=5, replica_groups=mesh['lat'=16,'dep'=8] {'lat','dep'}, dimensions={0}, use_global_device_ids=true | all-gather | bytes 528384 | tf_op jit(solution)/shard_map/all_gather | solution.py:153
  759.9 4.3 convolution_subtract_fusion.3
  767.2 63.2 %psum.68 = f32[5,32,32]{1,2,0:T(8,128)S(1)} all-reduce(f32[5,32,32]{1,2,0:T(8,128)S(1)} %fusion.76), channel_id=1, replica_groups=mesh['lat'=16,'dep'=8] {'lat','dep'}, use_global_device_ids=true, to_apply=%region_13.16 | all-reduce | flops 5120 | bytes 40960 | tf_op jit(solution)/shard_map/psum | solution.py:149
  835.9 38.7 %all-gather.4 = f32[4096,32]{1,0:T(8,128)} all-gather(f32[32,32]{1,0:T(8,128)S(1)} %convolution_bitcast_fusion.72), channel_id=6, replica_groups=mesh['lat'=16,'dep'=8] {'lat','dep'}, dimensions={0}, use_global_device_ids=true | all-gather | bytes 528384 | tf_op jit(solution)/shard_map/all_gather | solution.py:153
  912.3 4.3 convolution_subtract_fusion.2
  920.2 63.2 %psum.69 = f32[6,32,32]{1,2,0:T(8,128)S(1)} all-reduce(f32[6,32,32]{1,2,0:T(8,128)S(1)} %fusion.70), channel_id=1, replica_groups=mesh['lat'=16,'dep'=8] {'lat','dep'}, use_global_device_ids=true, to_apply=%region_15.18 | all-reduce | flops 6144 | bytes 49152 | tf_op jit(solution)/shard_map/psum | solution.py:149
  989.5 38.9 %all-gather.5 = f32[4096,32]{1,0:T(8,128)} all-gather(f32[32,32]{1,0:T(8,128)S(1)} %convolution_bitcast_fusion.64), channel_id=7, replica_groups=mesh['lat'=16,'dep'=8] {'lat','dep'}, dimensions={0}, use_global_device_ids=true | all-gather | bytes 528384 | tf_op jit(solution)/shard_map/all_gather | solution.py:153
  1067.0 4.3 convolution_subtract_fusion.1
  1075.5 63.2 %psum.70 = f32[7,32,32]{1,2,0:T(8,128)S(1)} all-reduce(f32[7,32,32]{1,2,0:T(8,128)S(1)} %fusion.63), channel_id=1, replica_groups=mesh['lat'=16,'dep'=8] {'lat','dep'}, use_global_device_ids=true, to_apply=%region_17.20 | all-reduce | flops 7168 | bytes 57344 | tf_op jit(solution)/shard_map/psum | solution.py:149
  1145.4 38.7 %all-gather.6 = f32[4096,32]{1,0:T(8,128)} all-gather(f32[32,32]{1,0:T(8,128)S(1)} %convolution_bitcast_fusion.55), channel_id=8, replica_groups=mesh['lat'=16,'dep'=8] {'lat','dep'}, dimensions={0}, use_global_device_ids=true | all-gather | bytes 528384 | tf_op jit(solution)/shard_map/all_gather | solution.py:153
  1228.4 62.9 %psum.71 = f32[8,32,32]{1,2,0:T(8,128)S(1)} all-reduce(f32[8,32,32]{1,2,0:T(8,128)S(1)} %fusion.55), channel_id=1, replica_groups=mesh['lat'=16,'dep'=8] {'lat','dep'}, use_global_device_ids=true, to_apply=%region_19.22 | all-reduce | flops 8192 | bytes 65536 | tf_op jit(solution)/shard_map/psum | solution.py:149
  1296.8 38.6 %all-gather.7 = f32[4096,32]{1,0:T(8,128)} all-gather(f32[32,32]{1,0:T(8,128)S(1)} %convolution_bitcast_fusion.45), channel_id=9, replica_groups=mesh['lat'=16,'dep'=8] {'lat','dep'}, dimensions={0}, use_global_device_ids=true | all-gather | bytes 528384 | tf_op jit(solution)/shard_map/all_gather | solution.py:153
  1350.8 11.7 cholesky.77
  1365.4 9.8 custom-call.23
  1377.4 11.9 cholesky.132
  1394.2 5.1 while.17
  1399.3 20.5 %custom-call.24 = f32[2,128,128]{1,2,0:T(8,128)S(1)} custom-call(f32[2,128,128]{2,1,0:T(8,128)} %get-tuple-element.122), custom_call_target="InvertDiagBlocksLowerTriangular" | custom-call | tf_op jit(solution)/shard_map/jit(_cho_solve)/triangular_solve | solution.py:173
  (685 shorter events, 445.3 us)
Async XLA Ops:
  79.2 84.8 %collective-permute-start = (f32[1,8,1024]{2,1,0:T(8,128)}, f32[1,8,1024]{2,1,0:T(8,128)}, u32[]{:S(2)}, u32[]{:S(2)}) collective-permute-start(f32[1,8,1024]{2,1,0:T(8,128)} %slice.619), channel_id=1, source_target_pairs={{0,8},{8,16},{16,24},{24,32},{32,40},{40,48},{48,56},{56,64},{64,7... | collective-permute-start | bytes 98312 | tf_op jit(solution)/shard_map/ppermute | solution.py:19
  79.9 85.6 %collective-permute-start.1 = (f32[1,8,1024]{2,1,0:T(8,128)}, f32[1,8,1024]{2,1,0:T(8,128)}, u32[]{:S(2)}, u32[]{:S(2)}) collective-permute-start(f32[1,8,1024]{2,1,0:T(8,128)} %slice.623), channel_id=1, source_target_pairs={{8,0},{16,8},{24,16},{32,24},{40,32},{48,40},{56,48},{64,56},{72,6... | collective-permute-start | bytes 98312 | tf_op jit(solution)/shard_map/ppermute | solution.py:21
  85.5 71.1 %collective-permute-start.2 = (f32[1,4,1024]{2,1,0:T(4,128)}, f32[1,4,1024]{2,1,0:T(4,128)S(1)}, u32[]{:S(2)}, u32[]{:S(2)}) collective-permute-start(f32[1,4,1024]{2,1,0:T(4,128)} %slice.625), channel_id=1, source_target_pairs={{0,1},{1,2},{2,3},{3,4},{4,5},{5,6},{6,7},{8,9},{9,10},{10,11},{11... | collective-permute-start | bytes 49160 | tf_op jit(solution)/shard_map/ppermute | solution.py:19
  89.2 73.4 %collective-permute-start.3 = (f32[1,4,1024]{2,1,0:T(4,128)}, f32[1,4,1024]{2,1,0:T(4,128)}, u32[]{:S(2)}, u32[]{:S(2)}) collective-permute-start(f32[1,4,1024]{2,1,0:T(4,128)} %slice.629), channel_id=1, source_target_pairs={{1,0},{2,1},{3,2},{4,3},{5,4},{6,5},{7,6},{9,8},{10,9},{11,10},{12... | collective-permute-start | bytes 49160 | tf_op jit(solution)/shard_map/ppermute | solution.py:21
  143.0 24.1 %collective-permute-start.4 = (f32[8,32,128]{2,1,0:T(8,128)}, f32[8,32,128]{2,1,0:T(8,128)}, u32[]{:S(2)}, u32[]{:S(2)}) collective-permute-start(f32[8,32,128]{2,1,0:T(8,128)} %broadcast_multiply_fusion.4), channel_id=1, source_target_pairs={{0,8},{8,16},{16,24},{24,32},{32,40},{40,48},{48,56},{56,64},{64,7... | collective-permute-start | bytes 393224 | tf_op jit(solution)/shard_map/ppermute | solution.py:31
  156.6 10.5 collective-permute-start.5
  298.5 14.6 %collective-permute-start.6 = (f32[1,8,1024]{2,1,0:T(8,128)}, f32[1,8,1024]{2,1,0:T(8,128)}, u32[]{:S(2)}, u32[]{:S(2)}) collective-permute-start(f32[1,8,1024]{2,1,0:T(8,128)} %slice.641), channel_id=1, source_target_pairs={{0,8},{8,16},{16,24},{24,32},{32,40},{40,48},{48,56},{56,64},{64,7... | collective-permute-start | bytes 98312 | tf_op jit(solution)/shard_map/ppermute | solution.py:19
  299.9 14.1 collective-permute-start.7
  304.1 5.4 collective-permute-start.8
  307.4 5.1 collective-permute-start.9
  444.1 16.5 %collective-permute-start.10 = (f32[1,8,1024]{2,1,0:T(8,128)}, f32[1,8,1024]{2,1,0:T(8,128)S(1)}, u32[]{:S(2)}, u32[]{:S(2)}) collective-permute-start(f32[1,8,1024]{2,1,0:T(8,128)} %slice.655), channel_id=1, source_target_pairs={{0,8},{8,16},{16,24},{24,32},{32,40},{40,48},{48,56},{56,64},{64,7... | collective-permute-start | bytes 98312 | tf_op jit(solution)/shard_map/ppermute | solution.py:19
  445.0 15.6 %collective-permute-start.11 = (f32[1,8,1024]{2,1,0:T(8,128)S(1)}, f32[1,8,1024]{2,1,0:T(8,128)}, u32[]{:S(2)}, u32[]{:S(2)}) collective-permute-start(f32[1,8,1024]{2,1,0:T(8,128)S(1)} %slice.659), channel_id=1, source_target_pairs={{8,0},{16,8},{24,16},{32,24},{40,32},{48,40},{56,48},{64,56},{72,6... | collective-permute-start | bytes 98312 | tf_op jit(solution)/shard_map/ppermute | solution.py:21
  450.0 9.1 collective-permute-start.12
  454.2 5.6 collective-permute-start.13
  592.5 15.8 %collective-permute-start.14 = (f32[1,8,1024]{2,1,0:T(8,128)}, f32[1,8,1024]{2,1,0:T(8,128)S(1)}, u32[]{:S(2)}, u32[]{:S(2)}) collective-permute-start(f32[1,8,1024]{2,1,0:T(8,128)} %slice.670), channel_id=1, source_target_pairs={{0,8},{8,16},{16,24},{24,32},{32,40},{40,48},{48,56},{56,64},{64,7... | collective-permute-start | bytes 98312 | tf_op jit(solution)/shard_map/ppermute | solution.py:19
  592.7 15.7 %collective-permute-start.15 = (f32[1,8,1024]{2,1,0:T(8,128)S(1)}, f32[1,8,1024]{2,1,0:T(8,128)}, u32[]{:S(2)}, u32[]{:S(2)}) collective-permute-start(f32[1,8,1024]{2,1,0:T(8,128)S(1)} %slice.674), channel_id=1, source_target_pairs={{8,0},{16,8},{24,16},{32,24},{40,32},{48,40},{56,48},{64,56},{72,6... | collective-permute-start | bytes 98312 | tf_op jit(solution)/shard_map/ppermute | solution.py:21
  598.3 8.5 collective-permute-start.16
  602.2 5.4 collective-permute-start.17
  742.7 15.5 %collective-permute-start.18 = (f32[1,8,1024]{2,1,0:T(8,128)}, f32[1,8,1024]{2,1,0:T(8,128)}, u32[]{:S(2)}, u32[]{:S(2)}) collective-permute-start(f32[1,8,1024]{2,1,0:T(8,128)} %slice.686), channel_id=1, source_target_pairs={{0,8},{8,16},{16,24},{24,32},{32,40},{40,48},{48,56},{56,64},{64,7... | collective-permute-start | bytes 98312 | tf_op jit(solution)/shard_map/ppermute | solution.py:19
  744.0 15.1 %collective-permute-start.19 = (f32[1,8,1024]{2,1,0:T(8,128)}, f32[1,8,1024]{2,1,0:T(8,128)}, u32[]{:S(2)}, u32[]{:S(2)}) collective-permute-start(f32[1,8,1024]{2,1,0:T(8,128)} %slice.690), channel_id=1, source_target_pairs={{8,0},{16,8},{24,16},{32,24},{40,32},{48,40},{56,48},{64,56},{72,6... | collective-permute-start | bytes 98312 | tf_op jit(solution)/shard_map/ppermute | solution.py:21
  749.1 7.5 collective-permute-start.20
  752.4 5.1 collective-permute-start.21
  894.2 16.4 %collective-permute-start.22 = (f32[1,8,1024]{2,1,0:T(8,128)S(1)}, f32[1,8,1024]{2,1,0:T(8,128)}, u32[]{:S(2)}, u32[]{:S(2)}) collective-permute-start(f32[1,8,1024]{2,1,0:T(8,128)S(1)} %slice.703), channel_id=1, source_target_pairs={{0,8},{8,16},{16,24},{24,32},{32,40},{40,48},{48,56},{56,64},{64,7... | collective-permute-start | bytes 98312 | tf_op jit(solution)/shard_map/ppermute | solution.py:19
  895.7 15.8 %collective-permute-start.23 = (f32[1,8,1024]{2,1,0:T(8,128)}, f32[1,8,1024]{2,1,0:T(8,128)}, u32[]{:S(2)}, u32[]{:S(2)}) collective-permute-start(f32[1,8,1024]{2,1,0:T(8,128)} %slice.707), channel_id=1, source_target_pairs={{8,0},{16,8},{24,16},{32,24},{40,32},{48,40},{56,48},{64,56},{72,6... | collective-permute-start | bytes 98312 | tf_op jit(solution)/shard_map/ppermute | solution.py:21
  900.7 8.0 collective-permute-start.24
  1048.8 16.5 %collective-permute-start.26 = (f32[1,8,1024]{2,1,0:T(8,128)S(1)}, f32[1,8,1024]{2,1,0:T(8,128)}, u32[]{:S(2)}, u32[]{:S(2)}) collective-permute-start(f32[1,8,1024]{2,1,0:T(8,128)S(1)} %slice.721), channel_id=1, source_target_pairs={{0,8},{8,16},{16,24},{24,32},{32,40},{40,48},{48,56},{56,64},{64,7... | collective-permute-start | bytes 98312 | tf_op jit(solution)/shard_map/ppermute | solution.py:19
  1050.3 15.8 %collective-permute-start.27 = (f32[1,8,1024]{2,1,0:T(8,128)}, f32[1,8,1024]{2,1,0:T(8,128)}, u32[]{:S(2)}, u32[]{:S(2)}) collective-permute-start(f32[1,8,1024]{2,1,0:T(8,128)} %slice.725), channel_id=1, source_target_pairs={{8,0},{16,8},{24,16},{32,24},{40,32},{48,40},{56,48},{64,56},{72,6... | collective-permute-start | bytes 98312 | tf_op jit(solution)/shard_map/ppermute | solution.py:21
  1055.3 7.0 collective-permute-start.28
  1059.5 5.1 collective-permute-start.29
  1203.9 15.2 %collective-permute-start.30 = (f32[1,8,1024]{2,1,0:T(8,128)S(1)}, f32[1,8,1024]{2,1,0:T(8,128)S(1)}, u32[]{:S(2)}, u32[]{:S(2)}) collective-permute-start(f32[1,8,1024]{2,1,0:T(8,128)S(1)} %slice.740), channel_id=1, source_target_pairs={{0,8},{8,16},{16,24},{24,32},{32,40},{40,48},{48,56},{56,64},{64,7... | collective-permute-start | bytes 98312 | tf_op jit(solution)/shard_map/ppermute | solution.py:19
  1204.8 14.5 %collective-permute-start.31 = (f32[1,8,1024]{2,1,0:T(8,128)S(1)}, f32[1,8,1024]{2,1,0:T(8,128)S(1)}, u32[]{:S(2)}, u32[]{:S(2)}) collective-permute-start(f32[1,8,1024]{2,1,0:T(8,128)S(1)} %slice.744), channel_id=1, source_target_pairs={{8,0},{16,8},{24,16},{32,24},{40,32},{48,40},{56,48},{64,56},{72,6... | collective-permute-start | bytes 98312 | tf_op jit(solution)/shard_map/ppermute | solution.py:21
  1209.9 7.7 collective-permute-start.32
  (93 other events, 754.7 us)
